TPU v7x, 32 devices: a whole 2x2x4 slice. The times are simulated.
32 devices in a mesh: cp: 8 (over z, x), dp: 4 (over y, core).
Axes of the slice: x: 2, y: 2, z: 4, core: 2. Of those that a mesh axis runs over, the one named last changes fastest.
Arguments:
- queries: bfloat16 [12288, 1024], P('cp', 'dp'), may hold values from -112 to 112, as said below
- keys: bfloat16 [12288, 128], P('cp'), may hold values from -7 to 7
- values: bfloat16 [12288, 128], P('cp'), may hold values from -6 to 6
- out_grad: bfloat16 [12288, 1024], P('cp', 'dp'), may hold values from -6 to 6
- lengths: int32 [24, 4], P('cp'), may hold values from 1 to 509, as said below
- hop_table: int32 [8, 3], P('cp'), may hold values from 0 to 2, each once within a row
Outputs:
- attn_out: bfloat16 [12288, 1024], P('cp', 'dp')
- query_grad: bfloat16 [12288, 1024], P('cp', 'dp')
- key_grad: bfloat16 [12288, 128], P('cp')
- value_grad: bfloat16 [12288, 128], P('cp')
- row_stats: float32 [8, 12288], P('dp', 'cp')
Inputs may be any that keep to these rules, and one draw needn't show every extreme that they name: Built so that queries and keys stay within this range. `lengths`: each row sums to 512; every slot of the first quarter of the cp loaders begins with a document of at least 384 rows. `hop_table`: each row names every hop once.
All inputs are finite; a program needn't handle non-finite values.
Results may differ from a plain program's by a relative error of at most 0.006.
Values may be sent and summed in bfloat16 or wider, within the bound.
A program may use at most 128 MiB of HBM per device.

v0:
```python
import functools
import math

import jax
import jax.numpy as jnp
from jax import lax
from jax.experimental import pallas as pl
from jax.experimental.pallas import tpu as pltpu
from jax.sharding import PartitionSpec as P

F32 = jnp.float32
BF16 = jnp.bfloat16
MESH = pl.DeviceIdType.MESH
LOWEST = -1e30


def nt(a, b):
    return lax.dot_general(a, b, (((1,), (1,)), ((), ())), preferred_element_type=F32)


def nn(a, b):
    return lax.dot_general(a, b, (((1,), (0,)), ((), ())), preferred_element_type=F32)


def kernel(
    sizes,
    len_ref,
    hop_ref,
    q_hbm,
    k_hbm,
    v_hbm,
    g_hbm,
    out_ref,
    qg_ref,
    kg_ref,
    vg_ref,
    rs_ref,
    q_v,
    k_v,
    v_v,
    g_v,
    own,
    part,
    precv,
    ysend,
    yrecv,
    fin,
    stats,
    ssend,
    srecv,
    in_sem,
    a_send,
    a_recv,
    b_send,
    b_recv,
    c_send,
    c_recv,
    s_send,
    s_recv,
):
    slots, rows, docs, heads, hd, tiles, cp_count, distances = sizes
    bq = rows // tiles
    half = bq // 2
    scale = hd ** (-0.5)
    c2 = scale * math.log2(math.e)
    cp = lax.axis_index("cp")
    dp = lax.axis_index("dp")
    side = lax.rem(dp, 2)
    outer = dp // 2
    mate = outer * 2 + (1 - side)
    across = (1 - outer) * 2 + side
    barrier = pltpu.get_barrier_semaphore()
    greeted = [{"cp": cp, "dp": mate}, {"cp": cp, "dp": across}]
    for distance in distances:
        greeted.append({"cp": lax.rem(cp + distance, cp_count), "dp": dp})
        greeted.append({"cp": lax.rem(cp + cp_count - distance, cp_count), "dp": dp})
    for target in greeted:
        pl.semaphore_signal(barrier, inc=1, device_id=target, device_id_type=MESH)

    def inputs(s):
        span = pl.ds(s * rows, rows)
        return [
            pltpu.make_async_copy(src.at[span], dst.at[span], in_sem.at[s, n])
            for n, (src, dst) in enumerate(
                ((k_hbm, k_v), (q_hbm, q_v), (v_hbm, v_v), (g_hbm, g_v))
            )
        ]

    for s in range(slots):
        for copy in inputs(s):
            copy.start()

    def to_mate(t):
        return pltpu.make_async_remote_copy(
            src_ref=part.at[t],
            dst_ref=precv.at[t],
            send_sem=a_send.at[t],
            recv_sem=a_recv.at[t],
            device_id={"cp": cp, "dp": mate},
            device_id_type=MESH,
        )

    def to_across(t):
        return pltpu.make_async_remote_copy(
            src_ref=ysend.at[t],
            dst_ref=yrecv.at[t],
            send_sem=b_send.at[t],
            recv_sem=b_recv.at[t],
            device_id={"cp": cp, "dp": across},
            device_id_type=MESH,
        )

    def first_row(t, which):
        s, i = t // tiles, tiles - 1 - t % tiles
        return pl.multiple_of(s * rows + i * bq + which * half, half)

    def shares(t):
        span = pl.ds(first_row(t, side), half)
        return [
            pltpu.make_async_remote_copy(
                src_ref=fin.at[t, n],
                dst_ref=dst.at[span],
                send_sem=c_send.at[t, n],
                recv_sem=c_recv.at[t, n],
                device_id={"cp": cp, "dp": mate},
                device_id_type=MESH,
            )
            for n, dst in enumerate((kg_ref, vg_ref))
        ]

    def stage_b(t):
        to_mate(t).wait_recv()
        ysend[t] = (own[t] + precv[t].astype(F32)).astype(BF16)
        to_across(t).start()

    def stage_c(t):
        to_across(t).wait_recv()
        total = (ysend[t].astype(F32) + yrecv[t].astype(F32)).astype(BF16)
        fin[t] = total
        span = pl.ds(first_row(t, side), half)
        kg_ref[span] = total[0]
        vg_ref[span] = total[1]
        for copy in shares(t):
            copy.start()

    count = slots * tiles
    for s in range(slots):
        for copy in inputs(s):
            copy.wait()
        base = s * rows
        position = lax.broadcasted_iota(jnp.int32, (1, rows), 1)
        start = jnp.zeros((1, rows), jnp.int32)
        end = 0
        for d in range(docs - 1):
            end = end + len_ref[s, d]
            start = jnp.where(position >= end, end, start)
        kt = k_v[base : base + rows].astype(F32).T.astype(BF16)
        vt = v_v[base : base + rows].astype(F32).T.astype(BF16)
        held_k = held_v = None
        for step in range(tiles):
            i = tiles - 1 - step
            t = s * tiles + step
            top = (i + 1) * bq
            k = k_v[base : base + top]
            v = v_v[base : base + top]
            low = i * bq
            key_pos = lax.broadcasted_iota(jnp.int32, (top, bq), 0)
            row_pos = lax.broadcasted_iota(jnp.int32, (top, bq), 1) + low
            allowed = (key_pos >= start[:, low:top]) & (key_pos <= row_pos)
            dk = dv = None
            for h in range(heads):
                lanes = slice(h * hd, (h + 1) * hd)
                q = q_v[base + low : base + top, lanes]
                g = g_v[base + low : base + top, lanes]
                scores = jnp.where(allowed, nt(k, q), LOWEST)
                high = jnp.max(scores, axis=0, keepdims=True)
                e = jnp.exp2((scores - high) * c2)
                total = jnp.sum(e, axis=0, keepdims=True)
                stats[s, h : h + 1, low:top] = high * scale + jnp.log(total)
                p = e * (1.0 / total)
                w = p.astype(BF16)
                pg = nt(v, g)
                delta = jnp.sum(p * pg, axis=0, keepdims=True)
                ds = (p * (pg - delta)).astype(BF16)
                out = nn(vt[:, :top], w)
                out_ref[base + low : base + top, lanes] = out.T.astype(BF16)
                qg = nn(kt[:, :top], ds) * scale
                qg_ref[base + low : base + top, lanes] = qg.T.astype(BF16)
                dv_h = nn(w, g)
                dk_h = nn(ds, q)
                dv = dv_h if dv is None else dv + dv_h
                dk = dk_h if dk is None else dk + dk_h
            if held_k is not None:
                dk = dk + held_k
                dv = dv + held_v
            held_k, held_v = dk[:low], dv[:low]
            dk = dk[low:] * scale
            dv = dv[low:]
            mine_low = side == 0
            own[t, 0] = jnp.where(mine_low, dk[:half], dk[half:])
            own[t, 1] = jnp.where(mine_low, dv[:half], dv[half:])
            part[t, 0] = jnp.where(mine_low, dk[half:], dk[:half]).astype(BF16)
            part[t, 1] = jnp.where(mine_low, dv[half:], dv[:half]).astype(BF16)
            if t == 0:
                pl.semaphore_wait(barrier, len(greeted))
            to_mate(t).start()
            if t >= 1:
                stage_b(t - 1)
            if t >= 3:
                stage_c(t - 3)

    def stat_copy(n):
        return pltpu.make_async_remote_copy(
            src_ref=ssend.at[n],
            dst_ref=srecv.at[n],
            send_sem=s_send.at[n],
            recv_sem=s_recv.at[n],
            device_id={"cp": lax.rem(cp + distances[n], cp_count), "dp": dp},
            device_id_type=MESH,
        )

    for hop in range(slots):
        piece = jnp.zeros((heads, rows), F32)
        for s in range(slots):
            piece = jnp.where(hop_ref[0, s] == hop, stats[s], piece)
        if hop == 0:
            rs_ref[:, 0:rows] = piece
        else:
            ssend[hop - 1] = piece
            stat_copy(hop - 1).start()
    stage_b(count - 1)
    for t in range(max(count - 3, 0), count):
        stage_c(t)
    for n in range(len(distances)):
        stat_copy(n).wait()
        rs_ref[:, (n + 1) * rows : (n + 2) * rows] = srecv[n]
    for t in range(count):
        to_mate(t).wait_send()
        to_across(t).wait_send()
        for copy in shares(t):
            copy.wait()


def local(cp_count, queries, keys, values, out_grad, lengths, hop_table):
    slots, docs = lengths.shape
    rows = queries.shape[0] // slots
    hd = keys.shape[1]
    heads = queries.shape[1] // hd
    tiles = 2
    distances = [cp_count >> (slots - hop) for hop in range(1, slots)]
    count = slots * tiles
    half = rows // tiles // 2
    piece = (count, 2, half, hd)
    sizes = (slots, rows, docs, heads, hd, tiles, cp_count, distances)
    dma = pltpu.SemaphoreType.DMA
    hops = len(distances)
    return tuple(
        pl.pallas_call(
            functools.partial(kernel, sizes),
            name="attend",
            out_shape=[
                jax.ShapeDtypeStruct(queries.shape, BF16),
                jax.ShapeDtypeStruct(queries.shape, BF16),
                jax.ShapeDtypeStruct(keys.shape, BF16),
                jax.ShapeDtypeStruct(values.shape, BF16),
                jax.ShapeDtypeStruct((heads, slots * rows), F32),
            ],
            in_specs=[pl.BlockSpec(memory_space=pltpu.SMEM)] * 2
            + [pl.BlockSpec(memory_space=pl.ANY)] * 4,
            out_specs=[pl.BlockSpec(memory_space=pltpu.VMEM)] * 5,
            scratch_shapes=[
                pltpu.VMEM(queries.shape, BF16),
                pltpu.VMEM(keys.shape, BF16),
                pltpu.VMEM(values.shape, BF16),
                pltpu.VMEM(out_grad.shape, BF16),
                pltpu.VMEM(piece, F32),
                pltpu.VMEM(piece, BF16),
                pltpu.VMEM(piece, BF16),
                pltpu.VMEM(piece, BF16),
                pltpu.VMEM(piece, BF16),
                pltpu.VMEM(piece, BF16),
                pltpu.VMEM((slots, heads, rows), F32),
                pltpu.VMEM((hops, heads, rows), F32),
                pltpu.VMEM((hops, heads, rows), F32),
                dma((slots, 4)),
                dma((count,)),
                dma((count,)),
                dma((count,)),
                dma((count,)),
                dma((count, 2)),
                dma((count, 2)),
                dma((hops,)),
                dma((hops,)),
            ],
            compiler_params=pltpu.CompilerParams(collective_id=0, has_side_effects=True),
        )(lengths, hop_table, queries, keys, values, out_grad)
    )


def solution(mesh):
    return jax.shard_map(
        functools.partial(local, mesh.shape["cp"]),
        mesh=mesh,
        in_specs=(
            P("cp", "dp"),
            P("cp", None),
            P("cp", None),
            P("cp", "dp"),
            P("cp", None),
            P("cp", None),
        ),
        out_specs=(P("cp", "dp"), P("cp", "dp"), P("cp", None), P("cp", None), P("dp", "cp")),
        check_vma=False,
    )
```

profile of v0, /device:TPU:0, one launch (start us, length us, event | category | flops | bytes accessed | tf_op | source)
XLA Modules:
  0.0 27.5 jit_solution(15511847378095525776)
XLA Ops:
  0.6 21.0 %attend.1 = (bf16[1536,256]{1,0:T(8,128)(2,1)}, bf16[1536,256]{1,0:T(8,128)(2,1)}, bf16[1536,128]{1,0:T(8,128)(2,1)}, bf16[1536,128]{1,0:T(8,128)(2,1)}, f32[2,1536]{1,0:T(2,128)}) custom-call(s32[3,4]{1,0:T(4,128)} %len_ref.1, s32[1,3]{1,0:T(1,128)} %hop_ref.1, bf16[1536,256]{1,0:T(8,128)(2,1)} %q_hbm.1, bf16[1536,128]{1,0:T(8,128)(2,1)} %k_hbm.1, ...), custom_call_target="tpu_custom_call" | custom-call | tf_op jit(solution)/shard_map/attend/pallas_call | solution.py:258
  21.6 0.0 copy-start
  21.6 2.1 %copy.16 = bf16[1536,256]{1,0:T(8,128)(2,1)} copy(bf16[1536,256]{1,0:T(8,128)(2,1)} %get-tuple-element.10) | data formatting | bytes 1572864
  23.8 0.0 copy-done
  23.8 0.0 copy-start.2
  23.8 0.9 %copy.17 = bf16[1536,256]{1,0:T(8,128)(2,1)} copy(bf16[1536,256]{1,0:T(8,128)(2,1)S(1)} %copy-done) | data formatting | bytes 1572864
  24.7 0.4 %copy-done.2 = bf16[1536,128]{1,0:T(8,128)(2,1)S(1)} copy-done((bf16[1536,128]{1,0:T(8,128)(2,1)S(1)}, bf16[1536,128]{1,0:T(8,128)(2,1)}, u32[]{:S(2)}) %copy-start.2) | copy-done | bytes 393240
  25.0 0.0 copy-start.1
  25.0 0.7 %copy.18 = bf16[1536,128]{1,0:T(8,128)(2,1)} copy(bf16[1536,128]{1,0:T(8,128)(2,1)S(1)} %copy-done.2) | data formatting | bytes 786432
  25.8 0.4 %copy-done.1 = bf16[1536,128]{1,0:T(8,128)(2,1)S(1)} copy-done((bf16[1536,128]{1,0:T(8,128)(2,1)S(1)}, bf16[1536,128]{1,0:T(8,128)(2,1)}, u32[]{:S(2)}) %copy-start.1) | copy-done | bytes 393240
  26.1 0.0 copy-start.3
  26.1 0.7 %copy.19 = bf16[1536,128]{1,0:T(8,128)(2,1)} copy(bf16[1536,128]{1,0:T(8,128)(2,1)S(1)} %copy-done.1) | data formatting | bytes 786432
  26.9 0.0 copy-done.3
  26.9 0.6 %copy.20 = f32[2,1536]{1,0:T(2,128)} copy(f32[2,1536]{1,0:T(2,128)S(1)} %copy-done.3) | data formatting | bytes 24576
Async XLA Ops:
  21.6 2.1 %copy-start = (bf16[1536,256]{1,0:T(8,128)(2,1)S(1)}, bf16[1536,256]{1,0:T(8,128)(2,1)}, u32[]{:S(2)}) copy-start(bf16[1536,256]{1,0:T(8,128)(2,1)} %get-tuple-element.11) | copy-start | bytes 2359300
  23.8 1.2 %copy-start.2 = (bf16[1536,128]{1,0:T(8,128)(2,1)S(1)}, bf16[1536,128]{1,0:T(8,128)(2,1)}, u32[]{:S(2)}) copy-start(bf16[1536,128]{1,0:T(8,128)(2,1)} %get-tuple-element.12) | copy-start | bytes 1179652
  25.0 1.1 %copy-start.1 = (bf16[1536,128]{1,0:T(8,128)(2,1)S(1)}, bf16[1536,128]{1,0:T(8,128)(2,1)}, u32[]{:S(2)}) copy-start(bf16[1536,128]{1,0:T(8,128)(2,1)} %get-tuple-element.13) | copy-start | bytes 1179652
  26.1 0.8 %copy-start.3 = (f32[2,1536]{1,0:T(2,128)S(1)}, f32[2,1536]{1,0:T(2,128)}, u32[]{:S(2)}) copy-start(f32[2,1536]{1,0:T(2,128)} %get-tuple-element.14) | copy-start | bytes 36868
where the time goes:
time: 27.8 us; the launch traced here: 27.5 us
  Pallas kernels  21 us (76%)
  local copies, waits for them, and re-layouts  5.86 us (21%)
  between operations  0.65 us (2%)
    pallas_call x1, Pallas kernels, local(): pl.pallas_call(functools.partial(kernel, sizes), name='attend', out_shape...  21 us
    unnamed x13, local copies, waits for them, and re-layouts  5.86 us

commit v1 on v0

--- a/solution.py
+++ b/solution.py
@@ -12,6 +12,7 @@
 BF16 = jnp.bfloat16
 MESH = pl.DeviceIdType.MESH
 LOWEST = -1e30
+LAG = 3
 
 
 def nt(a, b):
@@ -143,6 +144,14 @@
         for copy in shares(t):
             copy.start()
 
+    pending = []
+
+    def finish(left):
+        while len(pending) > left * heads:
+            span, lanes, vt, kt, w, ds = pending.pop(0)
+            out_ref[span, lanes] = nn(vt, w).T.astype(BF16)
+            qg_ref[span, lanes] = (nn(kt, ds) * scale).T.astype(BF16)
+
     count = slots * tiles
     for s in range(slots):
         for copy in inputs(s):
@@ -182,14 +191,12 @@
                 pg = nt(v, g)
                 delta = jnp.sum(p * pg, axis=0, keepdims=True)
                 ds = (p * (pg - delta)).astype(BF16)
-                out = nn(vt[:, :top], w)
-                out_ref[base + low : base + top, lanes] = out.T.astype(BF16)
-                qg = nn(kt[:, :top], ds) * scale
-                qg_ref[base + low : base + top, lanes] = qg.T.astype(BF16)
                 dv_h = nn(w, g)
                 dk_h = nn(ds, q)
                 dv = dv_h if dv is None else dv + dv_h
                 dk = dk_h if dk is None else dk + dk_h
+                span = slice(base + low, base + top)
+                pending.append((span, lanes, vt[:, :top], kt[:, :top], w, ds))
             if held_k is not None:
                 dk = dk + held_k
                 dv = dv + held_v
@@ -204,6 +211,7 @@
             if t == 0:
                 pl.semaphore_wait(barrier, len(greeted))
             to_mate(t).start()
+            finish(LAG)
             if t >= 1:
                 stage_b(t - 1)
             if t >= 3:
@@ -229,6 +237,7 @@
             ssend[hop - 1] = piece
             stat_copy(hop - 1).start()
     stage_b(count - 1)
+    finish(0)
     for t in range(max(count - 3, 0), count):
         stage_c(t)
     for n in range(len(distances)):
@@ -239,6 +248,18 @@
         to_across(t).wait_send()
         for copy in shares(t):
             copy.wait()
+
+
+def flush(*refs):
+    sem = refs[-1]
+    count = len(refs) // 2
+    copies = [
+        pltpu.make_async_copy(refs[n], refs[count + n], sem.at[n]) for n in range(count)
+    ]
+    for copy in copies:
+        copy.start()
+    for copy in copies:
+        copy.wait()
 
 
 def local(cp_count, queries, keys, values, out_grad, lengths, hop_table):
@@ -254,46 +275,55 @@
     sizes = (slots, rows, docs, heads, hd, tiles, cp_count, distances)
     dma = pltpu.SemaphoreType.DMA
     hops = len(distances)
+    results = [
+        (queries.shape, BF16),
+        (queries.shape, BF16),
+        (keys.shape, BF16),
+        (values.shape, BF16),
+        ((heads, slots * rows), F32),
+    ]
+    held = pl.pallas_call(
+        functools.partial(kernel, sizes),
+        name="attend",
+        out_shape=[pltpu.VMEM(*result) for result in results],
+        in_specs=[pl.BlockSpec(memory_space=pltpu.SMEM)] * 2
+        + [pl.BlockSpec(memory_space=pl.ANY)] * 4,
+        out_specs=[pl.BlockSpec(memory_space=pltpu.VMEM)] * 5,
+        scratch_shapes=[
+            pltpu.VMEM(queries.shape, BF16),
+            pltpu.VMEM(keys.shape, BF16),
+            pltpu.VMEM(values.shape, BF16),
+            pltpu.VMEM(out_grad.shape, BF16),
+            pltpu.VMEM(piece, F32),
+            pltpu.VMEM(piece, BF16),
+            pltpu.VMEM(piece, BF16),
+            pltpu.VMEM(piece, BF16),
+            pltpu.VMEM(piece, BF16),
+            pltpu.VMEM(piece, BF16),
+            pltpu.VMEM((slots, heads, rows), F32),
+            pltpu.VMEM((hops, heads, rows), F32),
+            pltpu.VMEM((hops, heads, rows), F32),
+            dma((slots, 4)),
+            dma((count,)),
+            dma((count,)),
+            dma((count,)),
+            dma((count,)),
+            dma((count, 2)),
+            dma((count, 2)),
+            dma((hops,)),
+            dma((hops,)),
+        ],
+        compiler_params=pltpu.CompilerParams(collective_id=0, has_side_effects=True),
+    )(lengths, hop_table, queries, keys, values, out_grad)
     return tuple(
         pl.pallas_call(
-            functools.partial(kernel, sizes),
-            name="attend",
-            out_shape=[
-                jax.ShapeDtypeStruct(queries.shape, BF16),
-                jax.ShapeDtypeStruct(queries.shape, BF16),
-                jax.ShapeDtypeStruct(keys.shape, BF16),
-                jax.ShapeDtypeStruct(values.shape, BF16),
-                jax.ShapeDtypeStruct((heads, slots * rows), F32),
-            ],
-            in_specs=[pl.BlockSpec(memory_space=pltpu.SMEM)] * 2
-            + [pl.BlockSpec(memory_space=pl.ANY)] * 4,
-            out_specs=[pl.BlockSpec(memory_space=pltpu.VMEM)] * 5,
-            scratch_shapes=[
-                pltpu.VMEM(queries.shape, BF16),
-                pltpu.VMEM(keys.shape, BF16),
-                pltpu.VMEM(values.shape, BF16),
-                pltpu.VMEM(out_grad.shape, BF16),
-                pltpu.VMEM(piece, F32),
-                pltpu.VMEM(piece, BF16),
-                pltpu.VMEM(piece, BF16),
-                pltpu.VMEM(piece, BF16),
-                pltpu.VMEM(piece, BF16),
-                pltpu.VMEM(piece, BF16),
-                pltpu.VMEM((slots, heads, rows), F32),
-                pltpu.VMEM((hops, heads, rows), F32),
-                pltpu.VMEM((hops, heads, rows), F32),
-                dma((slots, 4)),
-                dma((count,)),
-                dma((count,)),
-                dma((count,)),
-                dma((count,)),
-                dma((count, 2)),
-                dma((count, 2)),
-                dma((hops,)),
-                dma((hops,)),
-            ],
-            compiler_params=pltpu.CompilerParams(collective_id=0, has_side_effects=True),
-        )(lengths, hop_table, queries, keys, values, out_grad)
+            flush,
+            name="flush",
+            out_shape=[jax.ShapeDtypeStruct(*result) for result in results],
+            in_specs=[pl.BlockSpec(memory_space=pltpu.VMEM)] * 5,
+            out_specs=[pl.BlockSpec(memory_space=pl.ANY)] * 5,
+            scratch_shapes=[dma((5,))],
+        )(*[pltpu.with_memory_space_constraint(x, pltpu.VMEM) for x in held])
     )
 
 

time: 27.8 us -> 21.7 us (0.78)
  local copies, waits for them, and re-layouts: 5.86 us -> 0 us
    unnamed x13 -> x0, local copies, waits for them, and re-layouts: 5.86 us -> none
    pallas_call x1, Pallas kernels: 21 us -> 19.4 us  [local(): pl.pallas_call(functools.partial(kernel, sizes), name='attend', out_shape...]
    pallas_call x0 -> x1, Pallas kernels: none -> 1.44 us  [local(): pl.pallas_call(flush, name='flush', out_shape=[jax.ShapeDtypeStruct(*resu...]
where the time goes in v1:
time: 21.7 us; the launch traced here: 21.5 us
  Pallas kernels  20.9 us (96%)
  between operations  0.64 us (3%)
    pallas_call x1, Pallas kernels, local(): pl.pallas_call(functools.partial(kernel, sizes), name='attend', out_shape...  19.4 us
    pallas_call x1, Pallas kernels, local(): pl.pallas_call(flush, name='flush', out_shape=[jax.ShapeDtypeStruct(*resu...  1.44 us

profile of v1, /device:TPU:0, one launch (start us, length us, event | category | flops | bytes accessed | tf_op | source)
XLA Modules:
  0.0 21.5 jit_solution(10042642252159333718)
XLA Ops:
  0.6 19.4 %attend.1 = (bf16[1536,256]{1,0:T(8,128)(2,1)S(1)}, bf16[1536,256]{1,0:T(8,128)(2,1)S(1)}, bf16[1536,128]{1,0:T(8,128)(2,1)S(1)}, bf16[1536,128]{1,0:T(8,128)(2,1)S(1)}, f32[2,1536]{1,0:T(2,128)S(1)}) custom-call(s32[3,4]{1,0:T(4,128)} %len_ref.1, s32[1,3]{1,0:T(1,128)} %hop_ref.1, bf16[1536,256]{1,0:T(8,128)(2,1)} %q_hbm.1, bf16[1536,128]{1,0:T(8,128)(2,1)} %k_hbm.1, ...), custom_call_target="tpu_custom_call" | custom-call | tf_op jit(solution)/shard_map/attend/pallas_call | solution.py:285
  20.1 1.4 %flush.1 = (bf16[1536,256]{1,0:T(8,128)(2,1)}, bf16[1536,256]{1,0:T(8,128)(2,1)}, bf16[1536,128]{1,0:T(8,128)(2,1)}, bf16[1536,128]{1,0:T(8,128)(2,1)}, f32[2,1536]{1,0:T(2,128)}) custom-call(bf16[1536,256]{1,0:T(8,128)(2,1)S(1)} %get-tuple-element.10.refs_0_, bf16[1536,256]{1,0:T(8,128)(2,1)S(1)} %get-tuple-element.11.refs_1_, ...), custom_call_target="tpu_custom_call" | custom-call | tf_op jit(solution)/shard_map/flush/pallas_call | solution.py:319

commit v2 on v1

--- a/solution.py
+++ b/solution.py
@@ -12,7 +12,9 @@
 BF16 = jnp.bfloat16
 MESH = pl.DeviceIdType.MESH
 LOWEST = -1e30
-LAG = 3
+FINISH_LAG = 6
+PAIR_LAG = 2
+SHARE_LAG = 6
 
 
 def nt(a, b):
@@ -87,9 +89,8 @@
             )
         ]
 
-    for s in range(slots):
-        for copy in inputs(s):
-            copy.start()
+    for copy in inputs(0):
+        copy.start()
 
     def to_mate(t):
         return pltpu.make_async_remote_copy(
@@ -146,16 +147,28 @@
 
     pending = []
 
+    def side_by_side(ref, span):
+        return jnp.concatenate(
+            [ref[span, h * hd : (h + 1) * hd] for h in range(heads)], axis=0
+        )
+
     def finish(left):
-        while len(pending) > left * heads:
-            span, lanes, vt, kt, w, ds = pending.pop(0)
-            out_ref[span, lanes] = nn(vt, w).T.astype(BF16)
-            qg_ref[span, lanes] = (nn(kt, ds) * scale).T.astype(BF16)
+        while len(pending) > left:
+            span, vt, kt, w, ds = pending.pop(0)
+            out = nn(vt, w).T.astype(BF16)
+            qg = (nn(kt, ds) * scale).T.astype(BF16)
+            for h in range(heads):
+                out_ref[span, h * hd : (h + 1) * hd] = out[h * bq : (h + 1) * bq]
+                qg_ref[span, h * hd : (h + 1) * hd] = qg[h * bq : (h + 1) * bq]
 
     count = slots * tiles
     for s in range(slots):
         for copy in inputs(s):
             copy.wait()
+        if s == 0:
+            for later in range(1, slots):
+                for copy in inputs(later):
+                    copy.start()
         base = s * rows
         position = lax.broadcasted_iota(jnp.int32, (1, rows), 1)
         start = jnp.zeros((1, rows), jnp.int32)
@@ -176,27 +189,31 @@
             key_pos = lax.broadcasted_iota(jnp.int32, (top, bq), 0)
             row_pos = lax.broadcasted_iota(jnp.int32, (top, bq), 1) + low
             allowed = (key_pos >= start[:, low:top]) & (key_pos <= row_pos)
-            dk = dv = None
+            span = slice(base + low, base + top)
+            q = side_by_side(q_v, span)
+            g = side_by_side(g_v, span)
+            raw = nt(k, q)
+            scores = jnp.concatenate(
+                [
+                    jnp.where(allowed, raw[:, h * bq : (h + 1) * bq], LOWEST)
+                    for h in range(heads)
+                ],
+                axis=1,
+            )
+            high = jnp.max(scores, axis=0, keepdims=True)
+            e = jnp.exp2((scores - high) * c2)
+            total = jnp.sum(e, axis=0, keepdims=True)
+            stat = high * scale + jnp.log(total)
             for h in range(heads):
-                lanes = slice(h * hd, (h + 1) * hd)
-                q = q_v[base + low : base + top, lanes]
-                g = g_v[base + low : base + top, lanes]
-                scores = jnp.where(allowed, nt(k, q), LOWEST)
-                high = jnp.max(scores, axis=0, keepdims=True)
-                e = jnp.exp2((scores - high) * c2)
-                total = jnp.sum(e, axis=0, keepdims=True)
-                stats[s, h : h + 1, low:top] = high * scale + jnp.log(total)
-                p = e * (1.0 / total)
-                w = p.astype(BF16)
-                pg = nt(v, g)
-                delta = jnp.sum(p * pg, axis=0, keepdims=True)
-                ds = (p * (pg - delta)).astype(BF16)
-                dv_h = nn(w, g)
-                dk_h = nn(ds, q)
-                dv = dv_h if dv is None else dv + dv_h
-                dk = dk_h if dk is None else dk + dk_h
-                span = slice(base + low, base + top)
-                pending.append((span, lanes, vt[:, :top], kt[:, :top], w, ds))
+                stats[s, h : h + 1, low:top] = stat[:, h * bq : (h + 1) * bq]
+            p = e * (1.0 / total)
+            w = p.astype(BF16)
+            pg = nt(v, g)
+            delta = jnp.sum(p * pg, axis=0, keepdims=True)
+            ds = (p * (pg - delta)).astype(BF16)
+            dv = nn(w, g)
+            dk = nn(ds, q)
+            pending.append((span, vt[:, :top], kt[:, :top], w, ds))
             if held_k is not None:
                 dk = dk + held_k
                 dv = dv + held_v
@@ -211,11 +228,11 @@
             if t == 0:
                 pl.semaphore_wait(barrier, len(greeted))
             to_mate(t).start()
-            finish(LAG)
-            if t >= 1:
-                stage_b(t - 1)
-            if t >= 3:
-                stage_c(t - 3)
+            if t >= PAIR_LAG:
+                stage_b(t - PAIR_LAG)
+            finish(FINISH_LAG)
+            if t >= SHARE_LAG:
+                stage_c(t - SHARE_LAG)
 
     def stat_copy(n):
         return pltpu.make_async_remote_copy(
@@ -236,9 +253,11 @@
         else:
             ssend[hop - 1] = piece
             stat_copy(hop - 1).start()
-    stage_b(count - 1)
+    for t in range(count - PAIR_LAG, count):
+        finish(FINISH_LAG - 1 - (t - count + PAIR_LAG))
+        stage_b(t)
     finish(0)
-    for t in range(max(count - 3, 0), count):
+    for t in range(count - SHARE_LAG, count):
         stage_c(t)
     for n in range(len(distances)):
         stat_copy(n).wait()
@@ -267,7 +286,7 @@
     rows = queries.shape[0] // slots
     hd = keys.shape[1]
     heads = queries.shape[1] // hd
-    tiles = 2
+    tiles = 4
     distances = [cp_count >> (slots - hop) for hop in range(1, slots)]
     count = slots * tiles
     half = rows // tiles // 2

time: 21.7 us -> 23.1 us (1.065)
  Pallas kernels: 20.9 us -> 22.3 us
    pallas_call x1, Pallas kernels: 19.4 us -> 20.8 us  [local(): pl.pallas_call(functools.partial(kernel, sizes), name='attend', out_shape...]
where the time goes in v2:
time: 23.1 us; the launch traced here: 22.9 us
  Pallas kernels  22.3 us (97%)
  between operations  0.64 us (3%)
    pallas_call x1, Pallas kernels, local(): pl.pallas_call(functools.partial(kernel, sizes), name='attend', out_shape...  20.8 us
    pallas_call x1, Pallas kernels, local(): pl.pallas_call(flush, name='flush', out_shape=[jax.ShapeDtypeStruct(*resu...  1.44 us

profile of v2, /device:TPU:0, one launch (start us, length us, event | category | flops | bytes accessed | tf_op | source)
XLA Modules:
  0.0 22.9 jit_solution(16340037818215320618)
XLA Ops:
  0.6 20.8 %attend.1 = (bf16[1536,256]{1,0:T(8,128)(2,1)S(1)}, bf16[1536,256]{1,0:T(8,128)(2,1)S(1)}, bf16[1536,128]{1,0:T(8,128)(2,1)S(1)}, bf16[1536,128]{1,0:T(8,128)(2,1)S(1)}, f32[2,1536]{1,0:T(2,128)S(1)}) custom-call(s32[3,4]{1,0:T(4,128)} %len_ref.1, s32[1,3]{1,0:T(1,128)} %hop_ref.1, bf16[1536,256]{1,0:T(8,128)(2,1)} %q_hbm.1, bf16[1536,128]{1,0:T(8,128)(2,1)} %k_hbm.1, ...), custom_call_target="tpu_custom_call" | custom-call | tf_op jit(solution)/shard_map/attend/pallas_call | solution.py:304
  21.5 1.4 %flush.1 = (bf16[1536,256]{1,0:T(8,128)(2,1)}, bf16[1536,256]{1,0:T(8,128)(2,1)}, bf16[1536,128]{1,0:T(8,128)(2,1)}, bf16[1536,128]{1,0:T(8,128)(2,1)}, f32[2,1536]{1,0:T(2,128)}) custom-call(bf16[1536,256]{1,0:T(8,128)(2,1)S(1)} %get-tuple-element.10.refs_0_, bf16[1536,256]{1,0:T(8,128)(2,1)S(1)} %get-tuple-element.11.refs_1_, ...), custom_call_target="tpu_custom_call" | custom-call | tf_op jit(solution)/shard_map/flush/pallas_call | solution.py:338

commit v3 on v1

--- a/solution.py
+++ b/solution.py
@@ -25,8 +25,8 @@
 
 def kernel(
     sizes,
-    len_ref,
-    hop_ref,
+    len_hbm,
+    hop_hbm,
     q_hbm,
     k_hbm,
     v_hbm,
@@ -36,6 +36,8 @@
     kg_ref,
     vg_ref,
     rs_ref,
+    len_ref,
+    hop_ref,
     q_v,
     k_v,
     v_v,
@@ -50,6 +52,7 @@
     ssend,
     srecv,
     in_sem,
+    table_sem,
     a_send,
     a_recv,
     b_send,
@@ -71,10 +74,11 @@
     mate = outer * 2 + (1 - side)
     across = (1 - outer) * 2 + side
     barrier = pltpu.get_barrier_semaphore()
-    greeted = [{"cp": cp, "dp": mate}, {"cp": cp, "dp": across}]
-    for distance in distances:
+    greeted = []
+    for distance in reversed(distances):
         greeted.append({"cp": lax.rem(cp + distance, cp_count), "dp": dp})
         greeted.append({"cp": lax.rem(cp + cp_count - distance, cp_count), "dp": dp})
+    greeted += [{"cp": cp, "dp": across}, {"cp": cp, "dp": mate}]
     for target in greeted:
         pl.semaphore_signal(barrier, inc=1, device_id=target, device_id_type=MESH)
 
@@ -87,9 +91,14 @@
             )
         ]
 
-    for s in range(slots):
-        for copy in inputs(s):
-            copy.start()
+    tables = [
+        pltpu.make_async_copy(len_hbm, len_ref, table_sem.at[0]),
+        pltpu.make_async_copy(hop_hbm, hop_ref, table_sem.at[1]),
+    ]
+    for copy in tables + inputs(0):
+        copy.start()
+    for copy in tables:
+        copy.wait()
 
     def to_mate(t):
         return pltpu.make_async_remote_copy(
@@ -156,6 +165,10 @@
     for s in range(slots):
         for copy in inputs(s):
             copy.wait()
+        if s == 0:
+            for later in range(1, slots):
+                for copy in inputs(later):
+                    copy.start()
         base = s * rows
         position = lax.broadcasted_iota(jnp.int32, (1, rows), 1)
         start = jnp.zeros((1, rows), jnp.int32)
@@ -286,10 +299,11 @@
         functools.partial(kernel, sizes),
         name="attend",
         out_shape=[pltpu.VMEM(*result) for result in results],
-        in_specs=[pl.BlockSpec(memory_space=pltpu.SMEM)] * 2
-        + [pl.BlockSpec(memory_space=pl.ANY)] * 4,
+        in_specs=[pl.BlockSpec(memory_space=pl.ANY)] * 6,
         out_specs=[pl.BlockSpec(memory_space=pltpu.VMEM)] * 5,
         scratch_shapes=[
+            pltpu.SMEM(lengths.shape, jnp.int32),
+            pltpu.SMEM(hop_table.shape, jnp.int32),
             pltpu.VMEM(queries.shape, BF16),
             pltpu.VMEM(keys.shape, BF16),
             pltpu.VMEM(values.shape, BF16),
@@ -304,6 +318,7 @@
             pltpu.VMEM((hops, heads, rows), F32),
             pltpu.VMEM((hops, heads, rows), F32),
             dma((slots, 4)),
+            dma((2,)),
             dma((count,)),
             dma((count,)),
             dma((count,)),

time: 21.7 us -> 21 us (0.968)
  Pallas kernels: 20.9 us -> 20.2 us
    pallas_call x1, Pallas kernels: 19.4 us -> 18.7 us  [local(): pl.pallas_call(functools.partial(kernel, sizes), name='attend', out_shape...]
where the time goes in v3:
time: 21 us; the launch traced here: 20.8 us
  Pallas kernels  20.2 us (96%)
  between operations  0.64 us (3%)
    pallas_call x1, Pallas kernels, local(): pl.pallas_call(functools.partial(kernel, sizes), name='attend', out_shape...  18.7 us
    pallas_call x1, Pallas kernels, local(): pl.pallas_call(flush, name='flush', out_shape=[jax.ShapeDtypeStruct(*resu...  1.44 us

profile of v3, /device:TPU:0, one launch (start us, length us, event | category | flops | bytes accessed | tf_op | source)
XLA Modules:
  0.0 20.8 jit_solution(8436886599332829869)
XLA Ops:
  0.6 18.7 %attend.1 = (bf16[1536,256]{1,0:T(8,128)(2,1)S(1)}, bf16[1536,256]{1,0:T(8,128)(2,1)S(1)}, bf16[1536,128]{1,0:T(8,128)(2,1)S(1)}, bf16[1536,128]{1,0:T(8,128)(2,1)S(1)}, f32[2,1536]{1,0:T(2,128)S(1)}) custom-call(s32[3,4]{1,0:T(4,128)} %len_hbm.1, s32[1,3]{1,0:T(1,128)} %hop_hbm.1, bf16[1536,256]{1,0:T(8,128)(2,1)} %q_hbm.1, bf16[1536,128]{1,0:T(8,128)(2,1)} %k_hbm.1, ...), custom_call_target="tpu_custom_call" | custom-call | tf_op jit(solution)/shard_map/attend/pallas_call | solution.py:298
  19.4 1.4 %flush.1 = (bf16[1536,256]{1,0:T(8,128)(2,1)}, bf16[1536,256]{1,0:T(8,128)(2,1)}, bf16[1536,128]{1,0:T(8,128)(2,1)}, bf16[1536,128]{1,0:T(8,128)(2,1)}, f32[2,1536]{1,0:T(2,128)}) custom-call(bf16[1536,256]{1,0:T(8,128)(2,1)S(1)} %get-tuple-element.10.refs_0_, bf16[1536,256]{1,0:T(8,128)(2,1)S(1)} %get-tuple-element.11.refs_1_, ...), custom_call_target="tpu_custom_call" | custom-call | tf_op jit(solution)/shard_map/flush/pallas_call | solution.py:334
